TPU v7x, 128 devices: a whole 4x4x4 slice. The times are simulated.
128 devices in a mesh: sta: 8 (over x, y_hi), gx: 4 (over z), gy: 4 (over y_lo, core).
Axes of the slice: x: 4, y: 4 (y_hi: 2, y_lo: 2; y = y_hi * 2 + y_lo), z: 4, core: 2. Of those that a mesh axis runs over, the one named last changes fastest.
Arguments:
- rec_state: float32 [8, 4, 9, 32, 32, 128], P('sta', None, None, 'gx', 'gy'), may hold values from -6 to 6
- source_strain: bfloat16 [8, 8, 6, 32, 32, 128], P('sta', None, None, 'gx', 'gy'), may hold values from -6 to 6
- material: int32 [32, 32, 128], P('gx', 'gy'), may hold values from 0 to 15
- material_table: float32 [16, 3], replicated, may hold values from 0.5 to 1.5
- residual: float32 [8, 4, 8], P('sta'), may hold values from -4 to 4
- rec_cell: int32 [8, 4], P('sta'), may hold values from 0 to 1023
- listed: int32 [2, 8, 8], replicated, may hold values 0 or 1
- src_pick: int32 [2, 8], replicated, may hold values from 0 to 7
Outputs:
- kernels: float32 [2, 32, 32, 128], P(None, ('gx', 'sta'), 'gy')
All inputs are finite; a program needn't handle non-finite values.
Results may differ from a plain program's by a relative error of at most 0.0003.
Values may be sent and summed in bfloat16 or wider, within the bound.
A program may use at most 128 MiB of HBM per device.

v0:
```python
import jax
import jax.numpy as jnp
from jax import lax
from jax.sharding import PartitionSpec as P

C_NEAR = 8.0 / 12.0
C_FAR = -1.0 / 12.0
TIME_STEP = 0.25
AMPLITUDE = 4.0
KERNEL_SCALE = 0.0625
STIFFNESS = 0.3


def with_halo(block, sides, width):
    for axis, dim in sides:
        count = lax.axis_size(axis)
        forward = [(i, i + 1) for i in range(count - 1)]
        backward = [(target, source) for source, target in forward]
        low = lax.ppermute(
            lax.slice_in_dim(block, block.shape[dim] - width, None, axis=dim), axis, forward
        )
        high = lax.ppermute(lax.slice_in_dim(block, 0, width, axis=dim), axis, backward)
        block = jnp.concatenate([low, block, high], axis=dim)
    return block


def from_root(block, axis, source):
    block = jnp.where(lax.axis_index(axis) == source, block, jnp.zeros_like(block))
    return lax.psum(block, axis)


def along_first(padded):
    core = padded[..., :, 2:-2, 2:-2]
    return C_NEAR * (core[..., 3:-1, :, :] - core[..., 1:-3, :, :]) + C_FAR * (
        core[..., 4:, :, :] - core[..., :-4, :, :]
    )


def along_second(padded):
    core = padded[..., 2:-2, :, 2:-2]
    return C_NEAR * (core[..., :, 3:-1, :] - core[..., :, 1:-3, :]) + C_FAR * (
        core[..., :, 4:, :] - core[..., :, :-4, :]
    )


def along_depth(padded):
    core = padded[..., 2:-2, 2:-2, :]
    return C_NEAR * (core[..., 3:-1] - core[..., 1:-3]) + C_FAR * (core[..., 4:] - core[..., :-4])


def pad_depth(field):
    return jnp.pad(field, [(0, 0)] * (field.ndim - 1) + [(2, 2)])


def force_terms(padded, source_term):
    first = along_first(padded[:, 0]) + along_second(padded[:, 3]) + along_depth(padded[:, 4])
    second = along_first(padded[:, 3]) + along_second(padded[:, 1]) + along_depth(padded[:, 5])
    third = (
        along_first(padded[:, 4])
        + along_second(padded[:, 5])
        + along_depth(padded[:, 2])
        + source_term
    )
    return jnp.stack([first, second, third], 1)


def strain_rates(padded):
    comp_first = padded[:, 0]
    comp_second = padded[:, 1]
    comp_depth = padded[:, 2]
    rate_first = along_first(comp_first)
    rate_second = along_second(comp_second)
    rate_depth = along_depth(comp_depth)
    shear_plane = 0.5 * (along_second(comp_first) + along_first(comp_second))
    shear_first = 0.5 * (along_depth(comp_first) + along_first(comp_depth))
    shear_second = 0.5 * (along_depth(comp_second) + along_second(comp_depth))
    return jnp.stack(
        [rate_first, rate_second, rate_depth, shear_plane, shear_first, shear_second], 1
    )


def update_stress(stress, rates, lame, shear):
    trace = rates[:, 0] + rates[:, 1] + rates[:, 2]
    diagonal = stress[:, :3] + TIME_STEP * (lame * trace[:, None] + 2.0 * shear * rates[:, :3])
    offdiag = stress[:, 3:] + TIME_STEP * (2.0 * shear * rates[:, 3:])
    return jnp.concatenate([diagonal, offdiag], 1)


def correlate(source, weighted):
    trace_src = source[0] + source[1] + source[2]
    trace_rec = weighted[0] + weighted[1] + weighted[2]
    lam_part = trace_src * trace_rec
    diag_part = source[0] * weighted[0] + source[1] * weighted[1] + source[2] * weighted[2]
    off_part = source[3] * weighted[3] + source[4] * weighted[4] + source[5] * weighted[5]
    return jnp.stack([lam_part, 2.0 * diag_part + 4.0 * off_part])


def local(rec_state, source_strain, material, material_table, residual, rec_cell, listed, src_pick):
    state = rec_state[0]
    tile_x = state.shape[2]
    tile_y = state.shape[3]
    depth = state.shape[4]
    group = lax.axis_index("sta")
    count_mat = material_table.shape[0]
    onehot = (material[None] == jnp.arange(count_mat, dtype=jnp.int32)[:, None, None, None]).astype(
        jnp.float32
    )
    props = jnp.einsum("kxyz,kc->cxyz", onehot, material_table, precision=lax.Precision.HIGHEST)
    buoyancy = TIME_STEP / props[0]
    lame = STIFFNESS * props[1]
    shear = STIFFNESS * props[2]
    depth_first = (jnp.arange(depth) == 0).astype(jnp.float32)
    row_index = lax.axis_index("gx") * tile_x + jnp.arange(tile_x, dtype=jnp.int32)
    col_index = lax.axis_index("gy") * tile_y + jnp.arange(tile_y, dtype=jnp.int32)
    ny_total = lax.axis_size("gy") * tile_y
    cells = rec_cell[0]
    spots = ((cells // ny_total)[:, None, None] == row_index[None, :, None]) & (
        (cells % ny_total)[:, None, None] == col_index[None, None, :]
    )
    spots = spots.astype(jnp.float32)
    res_rows = residual[0]
    velocity = state[:, :3]
    stress = state[:, 3:]
    aggregates = []
    for moment in range(res_rows.shape[1]):
        source_term = (
            (AMPLITUDE * res_rows[:, moment])[:, None, None, None]
            * spots[:, :, :, None]
            * depth_first
        )
        stress_pad = pad_depth(with_halo(stress, (("gx", 2), ("gy", 3)), 2))
        velocity = velocity + buoyancy * force_terms(stress_pad, source_term)
        velocity_pad = pad_depth(with_halo(velocity, (("gx", 2), ("gy", 3)), 2))
        rates = strain_rates(velocity_pad)
        stress = update_stress(stress, rates, lame, shear)
        aggregates.append(
            jnp.sum((KERNEL_SCALE * res_rows[:, moment])[:, None, None, None, None] * rates, 0)
        )
    weights = lax.dynamic_slice_in_dim(listed, group, 1, 2)[:, :, 0].astype(jnp.float32)
    kernel = jnp.zeros((2, tile_x, tile_y, depth), jnp.float32)
    for rounds in range(listed.shape[0]):
        for moment in range(len(aggregates)):
            snaps = from_root(source_strain[0, moment], "sta", src_pick[rounds, moment])
            kernel = kernel + weights[rounds, moment] * correlate(
                snaps.astype(jnp.float32), aggregates[moment]
            )
    total = lax.psum(kernel, "sta")
    share = tile_x // lax.axis_size("sta")
    return lax.dynamic_slice_in_dim(total, group * share, share, 1)


def solution(mesh):
    in_specs = (
        P("sta", None, None, "gx", "gy", None),
        P("sta", None, None, "gx", "gy", None),
        P("gx", "gy", None),
        P(),
        P("sta", None, None),
        P("sta", None),
        P(),
        P(),
    )
    out_specs = P(None, ("gx", "sta"), "gy", None)
    return jax.shard_map(local, mesh=mesh, in_specs=in_specs, out_specs=out_specs, check_vma=False)
```

profile of v0, /device:TPU:0, one launch (start us, length us, event | category | flops | bytes accessed | tf_op | source)
XLA Modules:
  0.0 574.8 jit_solution(6821561108950658713)
XLA Ops:
  41.9 5.5 collective-permute-start.6
  62.2 4.4 collective-permute-done.9
  90.2 5.5 collective-permute-start.14
  108.8 4.4 collective-permute-done.17
  132.1 4.3 collective-permute-done.21
  136.5 5.5 collective-permute-start.22
  155.1 4.4 collective-permute-done.25
  178.4 4.3 collective-permute-done.29
  182.8 5.5 collective-permute-start.30
  201.4 4.4 collective-permute-done.33
  220.3 5.5 select_maximum_fusion.15
  252.6 4.5 collective-permute-start.40
  265.7 5.3 collective-permute-start.42
  274.1 73.0 %all-reduce.22.cloned.1.call-done = (bf16[6,8,8,128]{3,2,1,0:T(8,128)(2,1)}, bf16[6,8,8,128]{3,2,1,0:T(8,128)(2,1)}, bf16[6,8,8,128]{3,2,1,0:T(8,128)(2,1)}, bf1...) async-done(((bf16[6,8,8,128]{3,2,1,0:T(8,128)(2,1)}, ...) | async-done | bytes 1572880 | tf_op jit(solution)/shard_map/psum | solution.py:29
  349.0 5.8 %select_maximum_fusion.10 = f32[4,6,12,12,132]{4,3,2,0,1:T(8,128)S(1)} fusion(f32[4,6,12,2,128]{4,3,2,0,1:T(2,128)} %collective-permute-done.43, f32[4,6,12,2,128]{4,3,2,0,1:T(2,128)} %collective-permute-done.42, f32[4,6,2,8,128]{4,3,2,0,1:T(8,128)} %copy-done.20, f32[4,6,2,8,128]{4,3,2,0,1:T(8,128)S(1)} %collective-permute-done.40, ...), kind=kLoop, calls=%fused_computation.14 | loop fusion | flops 6386688 | bytes 3594240 | tf_op jit(solution)/shard_map/concatenate | solution.py:23
  363.3 4.3 collective-permute-done.45
  382.3 4.5 collective-permute-done.49
  407.1 4.3 collective-permute-done.53
  411.5 5.5 collective-permute-start.54
  429.4 4.4 collective-permute-done.57
  452.9 4.3 collective-permute-done.61
  457.3 5.5 collective-permute-start.62
  470.4 10.8 %fusion.647 = f32[2,8,8,128]{3,2,1,0:T(8,128)} fusion(f32[1,8,8,128]{3,2,1,0:T(8,128)S(1)} %get-tuple-element.290, f32[1,8,8,128]{3,2,1,0:T(8,128)S(1)} %get-tuple-element.289, f32[1,8,8,128]{3,2,1,0:T(8,128)S(1)} %get-tuple-element.286, f32[1,8,8,128]{3,2,1,0:T(8,128)S(1)} %get-tuple-element.285, f32[1,8,8,128]{3,2,1,0:T(8,128)S(1)} %get-tuple-element.282, ...), kind=kLoop, calls=%fused_computation.1256 | loop fusion | flops 770048 | bytes 1114176 | tf_op jit(solution)/shard_map/add | solution.py:144
  481.3 84.9 %all-reduce.20.cloned.1.call-done = f32[2,8,8,128]{3,2,1,0:T(8,128)} async-done(((f32[2,8,8,128]{3,2,1,0:T(8,128)}), f32[2,8,8,128]{3,2,1,0:T(8,128)}) %all-reduce.20.cloned.1.call-update) | async-done | bytes 65552 | tf_op jit(solution)/shard_map/psum | solution.py:147
  (434 shorter events, 276.9 us)
Async XLA Ops:
  6.5 340.5 %all-reduce.22.cloned.1.call-start = ((), (), s32[]{:S(2)}) async-start(), calls=%async_computation.1 | async-start | bytes 3145728 | tf_op jit(solution)/shard_map/psum | solution.py:29
  7.7 9.9 %collective-permute-start = (f32[4,6,2,8,128]{4,3,2,0,1:T(8,128)S(1)}, f32[4,6,2,8,128]{4,3,2,0,1:T(8,128)S(1)}, u32[]{:S(2)}, u32[]{:S(2)}) collective-permute-start(f32[4,6,2,8,128]{4,3,2,0,1:T(8,128)S(1)} %copy.59), channel_id=1, source_target_pairs={{0,4},{4,8},{8,12},{1,5},{5,9},{9,13},{2,6},{6,10},{10,14},{3,7},{... | collective-permute-start | bytes 589832 | tf_op jit(solution)/shard_map/ppermute | solution.py:19
  11.7 8.4 %collective-permute-start.1 = (f32[4,6,2,8,128]{4,3,2,0,1:T(8,128)S(1)}, f32[4,6,2,8,128]{4,3,2,0,1:T(8,128)S(1)}, u32[]{:S(2)}, u32[]{:S(2)}) collective-permute-start(f32[4,6,2,8,128]{4,3,2,0,1:T(8,128)S(1)} %copy.61), channel_id=1, source_target_pairs={{4,0},{8,4},{12,8},{5,1},{9,5},{13,9},{6,2},{10,6},{14,10},{7,3},{... | collective-permute-start | bytes 589832 | tf_op jit(solution)/shard_map/ppermute | solution.py:22
  41.9 6.9 %collective-permute-start.6 = (f32[4,3,12,2,128]{4,3,2,0,1:T(2,128)S(1)}, f32[4,3,12,2,128]{4,3,2,0,1:T(2,128)S(1)}, u32[]{:S(2)}, u32[]{:S(2)}) collective-permute-start(f32[4,3,12,2,128]{4,3,2,0,1:T(2,128)S(1)} %get-tuple-element.243), channel_id=1, source_target_pairs={{0,1},{1,2},{2,3},{4,5},{5,6},{6,7},{8,9},{9,10},{10,11},{12,13},{... | collective-permute-start | bytes 442376 | tf_op jit(solution)/shard_map/ppermute | solution.py:19
  59.0 7.6 %collective-permute-start.9 = (f32[4,6,2,8,128]{4,3,2,0,1:T(8,128)S(1)}, f32[4,6,2,8,128]{4,3,2,0,1:T(8,128)S(1)}, u32[]{:S(2)}, u32[]{:S(2)}) collective-permute-start(f32[4,6,2,8,128]{4,3,2,0,1:T(8,128)S(1)} %get-tuple-element.212), channel_id=1, source_target_pairs={{4,0},{8,4},{12,8},{5,1},{9,5},{13,9},{6,2},{10,6},{14,10},{7,3},{... | collective-permute-start | bytes 589832 | tf_op jit(solution)/shard_map/ppermute | solution.py:22
  90.2 6.9 %collective-permute-start.14 = (f32[4,3,12,2,128]{4,3,2,0,1:T(2,128)S(1)}, f32[4,3,12,2,128]{4,3,2,0,1:T(2,128)S(1)}, u32[]{:S(2)}, u32[]{:S(2)}) collective-permute-start(f32[4,3,12,2,128]{4,3,2,0,1:T(2,128)S(1)} %get-tuple-element.241), channel_id=1, source_target_pairs={{0,1},{1,2},{2,3},{4,5},{5,6},{6,7},{8,9},{9,10},{10,11},{12,13},{... | collective-permute-start | bytes 442376 | tf_op jit(solution)/shard_map/ppermute | solution.py:19
  105.7 7.6 %collective-permute-start.17 = (f32[4,6,2,8,128]{4,3,2,0,1:T(8,128)S(1)}, f32[4,6,2,8,128]{4,3,2,0,1:T(8,128)S(1)}, u32[]{:S(2)}, u32[]{:S(2)}) collective-permute-start(f32[4,6,2,8,128]{4,3,2,0,1:T(8,128)S(1)} %get-tuple-element.210), channel_id=1, source_target_pairs={{4,0},{8,4},{12,8},{5,1},{9,5},{13,9},{6,2},{10,6},{14,10},{7,3},{... | collective-permute-start | bytes 589832 | tf_op jit(solution)/shard_map/ppermute | solution.py:22
  136.5 6.9 %collective-permute-start.22 = (f32[4,3,12,2,128]{4,3,2,0,1:T(2,128)S(1)}, f32[4,3,12,2,128]{4,3,2,0,1:T(2,128)S(1)}, u32[]{:S(2)}, u32[]{:S(2)}) collective-permute-start(f32[4,3,12,2,128]{4,3,2,0,1:T(2,128)S(1)} %get-tuple-element.239), channel_id=1, source_target_pairs={{0,1},{1,2},{2,3},{4,5},{5,6},{6,7},{8,9},{9,10},{10,11},{12,13},{... | collective-permute-start | bytes 442376 | tf_op jit(solution)/shard_map/ppermute | solution.py:19
  151.9 7.6 %collective-permute-start.25 = (f32[4,6,2,8,128]{4,3,2,0,1:T(8,128)S(1)}, f32[4,6,2,8,128]{4,3,2,0,1:T(8,128)S(1)}, u32[]{:S(2)}, u32[]{:S(2)}) collective-permute-start(f32[4,6,2,8,128]{4,3,2,0,1:T(8,128)S(1)} %get-tuple-element.208), channel_id=1, source_target_pairs={{4,0},{8,4},{12,8},{5,1},{9,5},{13,9},{6,2},{10,6},{14,10},{7,3},{... | collective-permute-start | bytes 589832 | tf_op jit(solution)/shard_map/ppermute | solution.py:22
  182.8 6.9 %collective-permute-start.30 = (f32[4,3,12,2,128]{4,3,2,0,1:T(2,128)S(1)}, f32[4,3,12,2,128]{4,3,2,0,1:T(2,128)S(1)}, u32[]{:S(2)}, u32[]{:S(2)}) collective-permute-start(f32[4,3,12,2,128]{4,3,2,0,1:T(2,128)S(1)} %get-tuple-element.237), channel_id=1, source_target_pairs={{0,1},{1,2},{2,3},{4,5},{5,6},{6,7},{8,9},{9,10},{10,11},{12,13},{... | collective-permute-start | bytes 442376 | tf_op jit(solution)/shard_map/ppermute | solution.py:19
  198.2 7.6 %collective-permute-start.33 = (f32[4,6,2,8,128]{4,3,2,0,1:T(8,128)S(1)}, f32[4,6,2,8,128]{4,3,2,0,1:T(8,128)S(1)}, u32[]{:S(2)}, u32[]{:S(2)}) collective-permute-start(f32[4,6,2,8,128]{4,3,2,0,1:T(8,128)S(1)} %get-tuple-element.206), channel_id=1, source_target_pairs={{4,0},{8,4},{12,8},{5,1},{9,5},{13,9},{6,2},{10,6},{14,10},{7,3},{... | collective-permute-start | bytes 589832 | tf_op jit(solution)/shard_map/ppermute | solution.py:22
  206.8 13.4 %collective-permute-start.34 = (f32[4,6,12,2,128]{4,3,2,0,1:T(2,128)}, f32[4,6,12,2,128]{4,3,2,0,1:T(2,128)S(1)}, u32[]{:S(2)}, u32[]{:S(2)}) collective-permute-start(f32[4,6,12,2,128]{4,3,2,0,1:T(2,128)} %get-tuple-element.185), channel_id=1, source_target_pairs={{0,1},{1,2},{2,3},{4,5},{5,6},{6,7},{8,9},{9,10},{10,11},{12,13},{... | collective-permute-start | bytes 884744 | tf_op jit(solution)/shard_map/ppermute | solution.py:19
  211.0 9.3 %collective-permute-start.35 = (f32[4,6,12,2,128]{4,3,2,0,1:T(2,128)}, f32[4,6,12,2,128]{4,3,2,0,1:T(2,128)}, u32[]{:S(2)}, u32[]{:S(2)}) collective-permute-start(f32[4,6,12,2,128]{4,3,2,0,1:T(2,128)} %get-tuple-element.186), channel_id=1, source_target_pairs={{1,0},{2,1},{3,2},{5,4},{6,5},{7,6},{9,8},{10,9},{11,10},{13,12},{... | collective-permute-start | bytes 884744 | tf_op jit(solution)/shard_map/ppermute | solution.py:22
  228.9 8.8 %collective-permute-start.36 = (f32[4,3,2,8,128]{4,3,2,0,1:T(8,128)}, f32[4,3,2,8,128]{4,3,2,0,1:T(8,128)S(1)}, u32[]{:S(2)}, u32[]{:S(2)}) collective-permute-start(f32[4,3,2,8,128]{4,3,2,0,1:T(8,128)} %get-tuple-element.275), channel_id=1, source_target_pairs={{0,4},{4,8},{8,12},{1,5},{5,9},{9,13},{2,6},{6,10},{10,14},{3,7},{... | collective-permute-start | bytes 294920 | tf_op jit(solution)/shard_map/ppermute | solution.py:19
  231.1 7.2 %collective-permute-start.37 = (f32[4,3,2,8,128]{4,3,2,0,1:T(8,128)S(1)}, f32[4,3,2,8,128]{4,3,2,0,1:T(8,128)S(1)}, u32[]{:S(2)}, u32[]{:S(2)}) collective-permute-start(f32[4,3,2,8,128]{4,3,2,0,1:T(8,128)S(1)} %get-tuple-element.276), channel_id=1, source_target_pairs={{4,0},{8,4},{12,8},{5,1},{9,5},{13,9},{6,2},{10,6},{14,10},{7,3},{... | collective-permute-start | bytes 294920 | tf_op jit(solution)/shard_map/ppermute | solution.py:22
  245.9 320.3 %all-reduce.20.cloned.1.call-start = ((), (), s32[]{:S(2)}) async-start(), calls=%async_computation | async-start | bytes 131072 | tf_op jit(solution)/shard_map/psum | solution.py:147
  252.6 8.0 %collective-permute-start.40 = (f32[4,6,2,8,128]{4,3,2,0,1:T(8,128)}, f32[4,6,2,8,128]{4,3,2,0,1:T(8,128)S(1)}, u32[]{:S(2)}, u32[]{:S(2)}) collective-permute-start(f32[4,6,2,8,128]{4,3,2,0,1:T(8,128)} %get-tuple-element.203), channel_id=1, source_target_pairs={{0,4},{4,8},{8,12},{1,5},{5,9},{9,13},{2,6},{6,10},{10,14},{3,7},{... | collective-permute-start | bytes 589832 | tf_op jit(solution)/shard_map/ppermute | solution.py:19
  257.1 7.6 %collective-permute-start.41 = (f32[4,6,2,8,128]{4,3,2,0,1:T(8,128)S(1)}, f32[4,6,2,8,128]{4,3,2,0,1:T(8,128)S(1)}, u32[]{:S(2)}, u32[]{:S(2)}) collective-permute-start(f32[4,6,2,8,128]{4,3,2,0,1:T(8,128)S(1)} %get-tuple-element.204), channel_id=1, source_target_pairs={{4,0},{8,4},{12,8},{5,1},{9,5},{13,9},{6,2},{10,6},{14,10},{7,3},{... | collective-permute-start | bytes 589832 | tf_op jit(solution)/shard_map/ppermute | solution.py:22
  265.7 83.3 %collective-permute-start.42 = (f32[4,6,12,2,128]{4,3,2,0,1:T(2,128)}, f32[4,6,12,2,128]{4,3,2,0,1:T(2,128)}, u32[]{:S(2)}, u32[]{:S(2)}) collective-permute-start(f32[4,6,12,2,128]{4,3,2,0,1:T(2,128)} %get-tuple-element.183), channel_id=1, source_target_pairs={{0,1},{1,2},{2,3},{4,5},{5,6},{6,7},{8,9},{9,10},{10,11},{12,13},{... | collective-permute-start | bytes 884744 | tf_op jit(solution)/shard_map/ppermute | solution.py:19
  270.9 78.0 %collective-permute-start.43 = (f32[4,6,12,2,128]{4,3,2,0,1:T(2,128)}, f32[4,6,12,2,128]{4,3,2,0,1:T(2,128)}, u32[]{:S(2)}, u32[]{:S(2)}) collective-permute-start(f32[4,6,12,2,128]{4,3,2,0,1:T(2,128)} %get-tuple-element.184), channel_id=1, source_target_pairs={{1,0},{2,1},{3,2},{5,4},{6,5},{7,6},{9,8},{10,9},{11,10},{13,12},{... | collective-permute-start | bytes 884744 | tf_op jit(solution)/shard_map/ppermute | solution.py:22
  379.2 7.6 %collective-permute-start.49 = (f32[4,6,2,8,128]{4,3,2,0,1:T(8,128)S(1)}, f32[4,6,2,8,128]{4,3,2,0,1:T(8,128)S(1)}, u32[]{:S(2)}, u32[]{:S(2)}) collective-permute-start(f32[4,6,2,8,128]{4,3,2,0,1:T(8,128)S(1)} %get-tuple-element.202), channel_id=1, source_target_pairs={{4,0},{8,4},{12,8},{5,1},{9,5},{13,9},{6,2},{10,6},{14,10},{7,3},{... | collective-permute-start | bytes 589832 | tf_op jit(solution)/shard_map/ppermute | solution.py:22
  411.5 6.9 %collective-permute-start.54 = (f32[4,3,12,2,128]{4,3,2,0,1:T(2,128)S(1)}, f32[4,3,12,2,128]{4,3,2,0,1:T(2,128)S(1)}, u32[]{:S(2)}, u32[]{:S(2)}) collective-permute-start(f32[4,3,12,2,128]{4,3,2,0,1:T(2,128)S(1)} %get-tuple-element.231), channel_id=1, source_target_pairs={{0,1},{1,2},{2,3},{4,5},{5,6},{6,7},{8,9},{9,10},{10,11},{12,13},{... | collective-permute-start | bytes 442376 | tf_op jit(solution)/shard_map/ppermute | solution.py:19
  426.3 7.6 %collective-permute-start.57 = (f32[4,6,2,8,128]{4,3,2,1,0:T(8,128)S(1)}, f32[4,6,2,8,128]{4,3,2,1,0:T(8,128)S(1)}, u32[]{:S(2)}, u32[]{:S(2)}) collective-permute-start(f32[4,6,2,8,128]{4,3,2,1,0:T(8,128)S(1)} %get-tuple-element.200), channel_id=1, source_target_pairs={{4,0},{8,4},{12,8},{5,1},{9,5},{13,9},{6,2},{10,6},{14,10},{7,3},{... | collective-permute-start | bytes 589832 | tf_op jit(solution)/shard_map/ppermute | solution.py:22
  457.3 6.9 %collective-permute-start.62 = (f32[4,3,12,2,128]{4,3,2,0,1:T(2,128)S(1)}, f32[4,3,12,2,128]{4,3,2,0,1:T(2,128)S(1)}, u32[]{:S(2)}, u32[]{:S(2)}) collective-permute-start(f32[4,3,12,2,128]{4,3,2,0,1:T(2,128)S(1)} %get-tuple-element.229), channel_id=1, source_target_pairs={{0,1},{1,2},{2,3},{4,5},{5,6},{6,7},{8,9},{9,10},{10,11},{12,13},{... | collective-permute-start | bytes 442376 | tf_op jit(solution)/shard_map/ppermute | solution.py:19
  (92 other events, 809.4 us)
Sparse Core Ops, SparseCore 0:
  246.0 101.0 all-reduce.21
  481.4 84.7 all-reduce.19
where the time goes:
time: 585 us; the launch traced here: 575 us
  waiting for transfers between devices  275 us (47%)
  starting transfers between devices  157 us (27%)
  other arithmetic  96.7 us (17%)
  between operations  26.7 us (5%)
  local copies, waits for them, and re-layouts  18.2 us (3%)
    ppermute x32, starting transfers between devices, with_halo(): lax.ppermute(lax.slice_in_dim(block, block.shape[dim] - width, None, axis...  114 us
    ppermute x32, waiting for transfers between devices, with_halo(): lax.ppermute(lax.slice_in_dim(block, 0, width, axis=dim), axis, backward)  99.5 us
    psum x1, waiting for transfers between devices, local(): total = lax.psum(kernel, 'sta')  84.9 us
    psum x1, waiting for transfers between devices, from_root(): return lax.psum(block, axis)  73 us
    concatenate x16, other arithmetic, with_halo(): block = jnp.concatenate([low, block, high], axis=dim)  43.9 us
    ppermute x32, starting transfers between devices, with_halo(): lax.ppermute(lax.slice_in_dim(block, 0, width, axis=dim), axis, backward)  43.2 us
    ppermute x32, waiting for transfers between devices, with_halo(): lax.ppermute(lax.slice_in_dim(block, block.shape[dim] - width, None, axis...  17.8 us
  transfers between devices with their start and end apart: 66, of which 46 were waited for; matrix products, arithmetic and copies ran while one was open for 4% of the time, Pallas kernels for 0%

commit v1 on v0

--- a/solution.py
+++ b/solution.py
@@ -144,7 +144,11 @@
             kernel = kernel + weights[rounds, moment] * correlate(
                 snaps.astype(jnp.float32), aggregates[moment]
             )
-    total = lax.psum(kernel, "sta")
+
+    def cover_stops_all(arr_in, shard_axis):
+        return lax.all_gather(arr_in, axis_name=shard_axis).sum(axis=0)
+
+    total = cover_stops_all(kernel, "sta")
     share = tile_x // lax.axis_size("sta")
     return lax.dynamic_slice_in_dim(total, group * share, share, 1)
 

time: 585 us -> 536 us (0.916)
  the two profiles are of different devices: /device:TPU:0 before, /device:TPU:8 now
where the time goes in v1:
time: 536 us; the launch traced here: 526 us
  waiting for transfers between devices  194 us (36%)
  starting transfers between devices  155 us (29%)
  other arithmetic  96 us (18%)
  blocking collectives  35.2 us (7%)
  between operations  26.6 us (5%)
  local copies, waits for them, and re-layouts  17.5 us (3%)
    ppermute x32, waiting for transfers between devices, with_halo(): lax.ppermute(lax.slice_in_dim(block, 0, width, axis=dim), axis, backward)  86.9 us
    ppermute x32, starting transfers between devices, with_halo(): lax.ppermute(lax.slice_in_dim(block, 0, width, axis=dim), axis, backward)  80.8 us
    ppermute x32, starting transfers between devices, with_halo(): lax.ppermute(lax.slice_in_dim(block, block.shape[dim] - width, None, axis...  74.4 us
    psum x1, waiting for transfers between devices, from_root(): return lax.psum(block, axis)  70.7 us
    concatenate x16, other arithmetic, with_halo(): block = jnp.concatenate([low, block, high], axis=dim)  43.9 us
    ppermute x32, waiting for transfers between devices, with_halo(): lax.ppermute(lax.slice_in_dim(block, block.shape[dim] - width, None, axis...  36.7 us
    all_gather x1, blocking collectives, cover_stops_all(): return lax.all_gather(arr_in, axis_name=shard_axis).sum(axis=0)  35.2 us
    another operation x24, other arithmetic, force_terms(): return jnp.stack([first, second, third], 1)  10.9 us
  transfers between devices with their start and end apart: 65, of which 57 were waited for; matrix products, arithmetic and copies ran while one was open for 4% of the time, Pallas kernels for 0%

profile of v1, /device:TPU:8, one launch (start us, length us, event | category | flops | bytes accessed | tf_op | source)
XLA Modules:
  0.0 525.7 jit_solution(9666781851564022117)
XLA Ops:
  40.6 4.3 collective-permute-done.5
  63.9 4.4 collective-permute-done.9
  88.9 4.3 collective-permute-done.13
  110.6 4.4 collective-permute-done.17
  117.1 3.9 collective-permute-start.19
  135.2 4.3 collective-permute-done.21
  156.8 4.4 collective-permute-done.25
  163.4 4.1 collective-permute-start.27
  181.5 4.3 collective-permute-done.29
  203.2 4.4 collective-permute-done.33
  222.1 5.5 %select_maximum_fusion.15 = f32[4,6,12,12,132]{4,3,2,0,1:T(8,128)S(1)} fusion(f32[4,6,12,2,128]{4,3,2,0,1:T(2,128)} %collective-permute-done.35, f32[4,6,12,2,128]{4,3,2,0,1:T(2,128)S(1)} %collective-permute-done.34, f32[4,6,2,8,128]{4,3,2,0,1:T(8,128)S(1)} %collective-permute-done.33, f32[4,6,2,8,128]{4,3,2,0,1:T(8,128)S(1)} %collective-permute-done.32, ...), kind=kLoop, calls=%fused_computation.19 | loop fusion | flops 6386688 | bytes 3594240 | tf_op jit(solution)/shard_map/concatenate | solution.py:23
  254.3 4.5 collective-permute-start.40
  262.3 4.1 collective-permute-done.41
  274.9 70.7 %all-reduce.19.cloned.1.call-done = (bf16[6,8,8,128]{3,2,1,0:T(8,128)(2,1)}, bf16[6,8,8,128]{3,2,1,0:T(8,128)(2,1)}, bf16[6,8,8,128]{3,2,1,0:T(8,128)(2,1)}, bf1...) async-done(((bf16[6,8,8,128]{3,2,1,0:T(8,128)(2,1)}, ...) | async-done | bytes 1572880 | tf_op jit(solution)/shard_map/psum | solution.py:29
  347.5 5.8 %select_maximum_fusion.10 = f32[4,6,12,12,132]{4,3,2,0,1:T(8,128)S(1)} fusion(f32[4,6,12,2,128]{4,3,2,0,1:T(2,128)} %collective-permute-done.43, f32[4,6,12,2,128]{4,3,2,0,1:T(2,128)} %collective-permute-done.42, f32[4,6,2,8,128]{4,3,2,0,1:T(8,128)} %copy-done.20, f32[4,6,2,8,128]{4,3,2,0,1:T(8,128)S(1)} %collective-permute-done.40, ...), kind=kLoop, calls=%fused_computation.14 | loop fusion | flops 6386688 | bytes 3594240 | tf_op jit(solution)/shard_map/concatenate | solution.py:23
  361.4 4.3 collective-permute-done.45
  384.0 4.4 collective-permute-done.49
  390.6 3.9 collective-permute-start.51
  410.6 4.3 collective-permute-done.53
  431.5 4.4 collective-permute-done.57
  438.1 3.9 collective-permute-start.59
  456.4 4.3 collective-permute-done.61
  472.5 10.0 %fusion.647 = f32[1,2,8,8,128]{4,3,2,1,0:T(8,128)S(1)} fusion(f32[1,1,8,8,128]{4,3,2,1,0:T(8,128)S(1)} %get-tuple-element.290, f32[1,1,8,8,128]{4,3,2,1,0:T(8,128)S(1)} %get-tuple-element.289, f32[1,1,8,8,128]{4,3,2,1,0:T(8,128)S(1)} %get-tuple-element.286, f32[1,1,8,8,128]{4,3,2,1,0:T(8,128)S(1)} %get-tuple-element.285, ...), kind=kLoop, calls=%fused_computation.1256 | loop fusion | flops 770048 | bytes 1114176 | tf_op jit(solution)/shard_map/add | solution.py:144
  482.6 35.2 %all_gather.4 = f32[8,2,8,8,128]{4,3,2,1,0:T(8,128)S(1)} all-gather(f32[1,2,8,8,128]{4,3,2,1,0:T(8,128)S(1)} %fusion.647), channel_id=1, replica_groups=mesh['sta'=8,'gx'=4,'gy'=4] {'sta'}, dimensions={0}, use_global_device_ids=true | all-gather | bytes 589824 | tf_op jit(solution)/shard_map/all_gather | solution.py:149
  (433 shorter events, 290.7 us)
Async XLA Ops:
  6.5 339.1 %all-reduce.19.cloned.1.call-start = ((), (), s32[]{:S(2)}) async-start(), calls=%async_computation | async-start | bytes 3145728 | tf_op jit(solution)/shard_map/psum | solution.py:29
  7.7 9.9 %collective-permute-start = (f32[4,6,2,8,128]{4,3,2,0,1:T(8,128)S(1)}, f32[4,6,2,8,128]{4,3,2,0,1:T(8,128)S(1)}, u32[]{:S(2)}, u32[]{:S(2)}) collective-permute-start(f32[4,6,2,8,128]{4,3,2,0,1:T(8,128)S(1)} %copy.83), channel_id=1, source_target_pairs={{0,4},{4,8},{8,12},{1,5},{5,9},{9,13},{2,6},{6,10},{10,14},{3,7},{... | collective-permute-start | bytes 589832 | tf_op jit(solution)/shard_map/ppermute | solution.py:19
  11.6 8.4 %collective-permute-start.1 = (f32[4,6,2,8,128]{4,3,2,0,1:T(8,128)S(1)}, f32[4,6,2,8,128]{4,3,2,0,1:T(8,128)S(1)}, u32[]{:S(2)}, u32[]{:S(2)}) collective-permute-start(f32[4,6,2,8,128]{4,3,2,0,1:T(8,128)S(1)} %copy.85), channel_id=1, source_target_pairs={{4,0},{8,4},{12,8},{5,1},{9,5},{13,9},{6,2},{10,6},{14,10},{7,3},{... | collective-permute-start | bytes 589832 | tf_op jit(solution)/shard_map/ppermute | solution.py:22
  20.2 8.0 %collective-permute-start.2 = (f32[4,6,12,2,128]{4,3,2,0,1:T(2,128)S(1)}, f32[4,6,12,2,128]{4,3,2,0,1:T(2,128)S(1)}, u32[]{:S(2)}, u32[]{:S(2)}) collective-permute-start(f32[4,6,12,2,128]{4,3,2,0,1:T(2,128)S(1)} %get-tuple-element.195), channel_id=1, source_target_pairs={{0,1},{1,2},{2,3},{4,5},{5,6},{6,7},{8,9},{9,10},{10,11},{12,13},{... | collective-permute-start | bytes 884744 | tf_op jit(solution)/shard_map/ppermute | solution.py:19
  22.2 7.9 %collective-permute-start.3 = (f32[4,6,12,2,128]{4,3,2,0,1:T(2,128)S(1)}, f32[4,6,12,2,128]{4,3,2,0,1:T(2,128)S(1)}, u32[]{:S(2)}, u32[]{:S(2)}) collective-permute-start(f32[4,6,12,2,128]{4,3,2,0,1:T(2,128)S(1)} %get-tuple-element.196), channel_id=1, source_target_pairs={{1,0},{2,1},{3,2},{5,4},{6,5},{7,6},{9,8},{10,9},{11,10},{13,12},{... | collective-permute-start | bytes 884744 | tf_op jit(solution)/shard_map/ppermute | solution.py:22
  60.8 7.6 %collective-permute-start.9 = (f32[4,6,2,8,128]{4,3,2,0,1:T(8,128)S(1)}, f32[4,6,2,8,128]{4,3,2,0,1:T(8,128)S(1)}, u32[]{:S(2)}, u32[]{:S(2)}) collective-permute-start(f32[4,6,2,8,128]{4,3,2,0,1:T(8,128)S(1)} %get-tuple-element.212), channel_id=1, source_target_pairs={{4,0},{8,4},{12,8},{5,1},{9,5},{13,9},{6,2},{10,6},{14,10},{7,3},{... | collective-permute-start | bytes 589832 | tf_op jit(solution)/shard_map/ppermute | solution.py:22
  68.5 8.0 %collective-permute-start.10 = (f32[4,6,12,2,128]{4,3,2,0,1:T(2,128)S(1)}, f32[4,6,12,2,128]{4,3,2,0,1:T(2,128)S(1)}, u32[]{:S(2)}, u32[]{:S(2)}) collective-permute-start(f32[4,6,12,2,128]{4,3,2,0,1:T(2,128)S(1)} %get-tuple-element.191), channel_id=1, source_target_pairs={{0,1},{1,2},{2,3},{4,5},{5,6},{6,7},{8,9},{9,10},{10,11},{12,13},{... | collective-permute-start | bytes 884744 | tf_op jit(solution)/shard_map/ppermute | solution.py:19
  70.4 7.9 %collective-permute-start.11 = (f32[4,6,12,2,128]{4,3,2,0,1:T(2,128)S(1)}, f32[4,6,12,2,128]{4,3,2,0,1:T(2,128)S(1)}, u32[]{:S(2)}, u32[]{:S(2)}) collective-permute-start(f32[4,6,12,2,128]{4,3,2,0,1:T(2,128)S(1)} %get-tuple-element.192), channel_id=1, source_target_pairs={{1,0},{2,1},{3,2},{5,4},{6,5},{7,6},{9,8},{10,9},{11,10},{13,12},{... | collective-permute-start | bytes 884744 | tf_op jit(solution)/shard_map/ppermute | solution.py:22
  107.4 7.6 %collective-permute-start.17 = (f32[4,6,2,8,128]{4,3,2,0,1:T(8,128)S(1)}, f32[4,6,2,8,128]{4,3,2,0,1:T(8,128)S(1)}, u32[]{:S(2)}, u32[]{:S(2)}) collective-permute-start(f32[4,6,2,8,128]{4,3,2,0,1:T(8,128)S(1)} %get-tuple-element.210), channel_id=1, source_target_pairs={{4,0},{8,4},{12,8},{5,1},{9,5},{13,9},{6,2},{10,6},{14,10},{7,3},{... | collective-permute-start | bytes 589832 | tf_op jit(solution)/shard_map/ppermute | solution.py:22
  115.2 8.0 %collective-permute-start.18 = (f32[4,6,12,2,128]{4,3,2,0,1:T(2,128)S(1)}, f32[4,6,12,2,128]{4,3,2,0,1:T(2,128)S(1)}, u32[]{:S(2)}, u32[]{:S(2)}) collective-permute-start(f32[4,6,12,2,128]{4,3,2,0,1:T(2,128)S(1)} %get-tuple-element.189), channel_id=1, source_target_pairs={{0,1},{1,2},{2,3},{4,5},{5,6},{6,7},{8,9},{9,10},{10,11},{12,13},{... | collective-permute-start | bytes 884744 | tf_op jit(solution)/shard_map/ppermute | solution.py:19
  117.1 7.9 %collective-permute-start.19 = (f32[4,6,12,2,128]{4,3,2,0,1:T(2,128)S(1)}, f32[4,6,12,2,128]{4,3,2,0,1:T(2,128)S(1)}, u32[]{:S(2)}, u32[]{:S(2)}) collective-permute-start(f32[4,6,12,2,128]{4,3,2,0,1:T(2,128)S(1)} %get-tuple-element.190), channel_id=1, source_target_pairs={{1,0},{2,1},{3,2},{5,4},{6,5},{7,6},{9,8},{10,9},{11,10},{13,12},{... | collective-permute-start | bytes 884744 | tf_op jit(solution)/shard_map/ppermute | solution.py:22
  161.4 8.0 %collective-permute-start.26 = (f32[4,6,12,2,128]{4,3,2,0,1:T(2,128)S(1)}, f32[4,6,12,2,128]{4,3,2,0,1:T(2,128)S(1)}, u32[]{:S(2)}, u32[]{:S(2)}) collective-permute-start(f32[4,6,12,2,128]{4,3,2,0,1:T(2,128)S(1)} %get-tuple-element.187), channel_id=1, source_target_pairs={{0,1},{1,2},{2,3},{4,5},{5,6},{6,7},{8,9},{9,10},{10,11},{12,13},{... | collective-permute-start | bytes 884744 | tf_op jit(solution)/shard_map/ppermute | solution.py:19
  163.4 7.9 %collective-permute-start.27 = (f32[4,6,12,2,128]{4,3,2,0,1:T(2,128)S(1)}, f32[4,6,12,2,128]{4,3,2,0,1:T(2,128)S(1)}, u32[]{:S(2)}, u32[]{:S(2)}) collective-permute-start(f32[4,6,12,2,128]{4,3,2,0,1:T(2,128)S(1)} %get-tuple-element.188), channel_id=1, source_target_pairs={{1,0},{2,1},{3,2},{5,4},{6,5},{7,6},{9,8},{10,9},{11,10},{13,12},{... | collective-permute-start | bytes 884744 | tf_op jit(solution)/shard_map/ppermute | solution.py:22
  208.6 13.5 %collective-permute-start.34 = (f32[4,6,12,2,128]{4,3,2,0,1:T(2,128)}, f32[4,6,12,2,128]{4,3,2,0,1:T(2,128)S(1)}, u32[]{:S(2)}, u32[]{:S(2)}) collective-permute-start(f32[4,6,12,2,128]{4,3,2,0,1:T(2,128)} %get-tuple-element.185), channel_id=1, source_target_pairs={{0,1},{1,2},{2,3},{4,5},{5,6},{6,7},{8,9},{9,10},{10,11},{12,13},{... | collective-permute-start | bytes 884744 | tf_op jit(solution)/shard_map/ppermute | solution.py:19
  210.5 11.6 %collective-permute-start.35 = (f32[4,6,12,2,128]{4,3,2,0,1:T(2,128)}, f32[4,6,12,2,128]{4,3,2,0,1:T(2,128)}, u32[]{:S(2)}, u32[]{:S(2)}) collective-permute-start(f32[4,6,12,2,128]{4,3,2,0,1:T(2,128)} %get-tuple-element.186), channel_id=1, source_target_pairs={{1,0},{2,1},{3,2},{5,4},{6,5},{7,6},{9,8},{10,9},{11,10},{13,12},{... | collective-permute-start | bytes 884744 | tf_op jit(solution)/shard_map/ppermute | solution.py:22
  230.7 8.6 %collective-permute-start.36 = (f32[4,3,2,8,128]{4,3,2,0,1:T(8,128)}, f32[4,3,2,8,128]{4,3,2,0,1:T(8,128)S(1)}, u32[]{:S(2)}, u32[]{:S(2)}) collective-permute-start(f32[4,3,2,8,128]{4,3,2,0,1:T(8,128)} %get-tuple-element.275), channel_id=1, source_target_pairs={{0,4},{4,8},{8,12},{1,5},{5,9},{9,13},{2,6},{6,10},{10,14},{3,7},{... | collective-permute-start | bytes 294920 | tf_op jit(solution)/shard_map/ppermute | solution.py:19
  240.2 7.7 %collective-permute-start.38 = (f32[4,3,12,2,128]{4,3,2,0,1:T(2,128)}, f32[4,3,12,2,128]{4,3,2,0,1:T(2,128)}, u32[]{:S(2)}, u32[]{:S(2)}) collective-permute-start(f32[4,3,12,2,128]{4,3,2,0,1:T(2,128)} %get-tuple-element.235), channel_id=1, source_target_pairs={{0,1},{1,2},{2,3},{4,5},{5,6},{6,7},{8,9},{9,10},{10,11},{12,13},{... | collective-permute-start | bytes 442376 | tf_op jit(solution)/shard_map/ppermute | solution.py:19
  254.3 8.0 %collective-permute-start.40 = (f32[4,6,2,8,128]{4,3,2,0,1:T(8,128)}, f32[4,6,2,8,128]{4,3,2,0,1:T(8,128)S(1)}, u32[]{:S(2)}, u32[]{:S(2)}) collective-permute-start(f32[4,6,2,8,128]{4,3,2,0,1:T(8,128)} %get-tuple-element.203), channel_id=1, source_target_pairs={{0,4},{4,8},{8,12},{1,5},{5,9},{9,13},{2,6},{6,10},{10,14},{3,7},{... | collective-permute-start | bytes 589832 | tf_op jit(solution)/shard_map/ppermute | solution.py:19
  267.4 80.0 %collective-permute-start.42 = (f32[4,6,12,2,128]{4,3,2,0,1:T(2,128)}, f32[4,6,12,2,128]{4,3,2,0,1:T(2,128)}, u32[]{:S(2)}, u32[]{:S(2)}) collective-permute-start(f32[4,6,12,2,128]{4,3,2,0,1:T(2,128)} %get-tuple-element.183), channel_id=1, source_target_pairs={{0,1},{1,2},{2,3},{4,5},{5,6},{6,7},{8,9},{9,10},{10,11},{12,13},{... | collective-permute-start | bytes 884744 | tf_op jit(solution)/shard_map/ppermute | solution.py:19
  269.4 78.1 %collective-permute-start.43 = (f32[4,6,12,2,128]{4,3,2,0,1:T(2,128)}, f32[4,6,12,2,128]{4,3,2,0,1:T(2,128)}, u32[]{:S(2)}, u32[]{:S(2)}) collective-permute-start(f32[4,6,12,2,128]{4,3,2,0,1:T(2,128)} %get-tuple-element.184), channel_id=1, source_target_pairs={{1,0},{2,1},{3,2},{5,4},{6,5},{7,6},{9,8},{10,9},{11,10},{13,12},{... | collective-permute-start | bytes 884744 | tf_op jit(solution)/shard_map/ppermute | solution.py:22
  388.6 8.0 %collective-permute-start.50 = (f32[4,6,12,2,128]{4,3,2,0,1:T(2,128)S(1)}, f32[4,6,12,2,128]{4,3,2,0,1:T(2,128)S(1)}, u32[]{:S(2)}, u32[]{:S(2)}) collective-permute-start(f32[4,6,12,2,128]{4,3,2,0,1:T(2,128)S(1)} %get-tuple-element.181), channel_id=1, source_target_pairs={{0,1},{1,2},{2,3},{4,5},{5,6},{6,7},{8,9},{9,10},{10,11},{12,13},{... | collective-permute-start | bytes 884744 | tf_op jit(solution)/shard_map/ppermute | solution.py:19
  390.6 7.9 %collective-permute-start.51 = (f32[4,6,12,2,128]{4,3,2,0,1:T(2,128)S(1)}, f32[4,6,12,2,128]{4,3,2,0,1:T(2,128)S(1)}, u32[]{:S(2)}, u32[]{:S(2)}) collective-permute-start(f32[4,6,12,2,128]{4,3,2,0,1:T(2,128)S(1)} %get-tuple-element.182), channel_id=1, source_target_pairs={{1,0},{2,1},{3,2},{5,4},{6,5},{7,6},{9,8},{10,9},{11,10},{13,12},{... | collective-permute-start | bytes 884744 | tf_op jit(solution)/shard_map/ppermute | solution.py:22
  436.1 8.0 %collective-permute-start.58 = (f32[4,6,12,2,128]{4,3,2,1,0:T(2,128)S(1)}, f32[4,6,12,2,128]{4,3,2,1,0:T(2,128)S(1)}, u32[]{:S(2)}, u32[]{:S(2)}) collective-permute-start(f32[4,6,12,2,128]{4,3,2,1,0:T(2,128)S(1)} %get-tuple-element.179), channel_id=1, source_target_pairs={{0,1},{1,2},{2,3},{4,5},{5,6},{6,7},{8,9},{9,10},{10,11},{12,13},{... | collective-permute-start | bytes 884744 | tf_op jit(solution)/shard_map/ppermute | solution.py:19
  438.1 7.9 %collective-permute-start.59 = (f32[4,6,12,2,128]{4,3,2,1,0:T(2,128)S(1)}, f32[4,6,12,2,128]{4,3,2,1,0:T(2,128)S(1)}, u32[]{:S(2)}, u32[]{:S(2)}) collective-permute-start(f32[4,6,12,2,128]{4,3,2,1,0:T(2,128)S(1)} %get-tuple-element.180), channel_id=1, source_target_pairs={{1,0},{2,1},{3,2},{5,4},{6,5},{7,6},{9,8},{10,9},{11,10},{13,12},{... | collective-permute-start | bytes 884744 | tf_op jit(solution)/shard_map/ppermute | solution.py:22
  (91 other events, 787.9 us)
Sparse Core Ops, SparseCore 0:
  248.0 97.6 all-reduce.18
